TPU v7x, 32 devices: a whole 2x2x4 slice. The times are simulated.
32 devices in a mesh: fsdp: 8 (over z, y), rep: 4 (over x, core).
Axes of the slice: x: 2, y: 2, z: 4, core: 2. Of those that a mesh axis runs over, the one named last changes fastest.
Arguments:
- layer_input: bfloat16 [64, 512, 768], P(('fsdp', 'rep')), may hold values from -6 to 6
- segment_ids: int32 [64, 512], P(('fsdp', 'rep')), may hold values from 0 to 511, as said below
- joint_weight: bfloat16 [768, 2304], P('fsdp'), may hold values from -0.21875 to 0.21875
- query_bias: bfloat16 [768], replicated, may hold values from -3 to 3
- value_bias: bfloat16 [768], replicated, may hold values from -3 to 3
- close_weight: bfloat16 [768, 768], P('fsdp'), may hold values from -0.875 to 0.875
- close_bias: bfloat16 [768], replicated, may hold values from -3 to 3
- first_gain: bfloat16 [768], replicated, may hold values from 0.099609375 to 1.8984375
- first_shift: bfloat16 [768], replicated, may hold values from -3 to 3
- expand_weight: bfloat16 [768, 3072], P('fsdp'), may hold values from -0.21875 to 0.21875
- expand_bias: bfloat16 [3072], replicated, may hold values from -3 to 3
- shrink_weight: bfloat16 [3072, 768], P('fsdp'), may hold values from -0.109375 to 0.109375
- shrink_bias: bfloat16 [768], replicated, may hold values from -3 to 3
- second_gain: bfloat16 [768], replicated, may hold values from 0.099609375 to 1.8984375
- second_shift: bfloat16 [768], replicated, may hold values from -3 to 3
- cotangent: bfloat16 [64, 512, 768], P(('fsdp', 'rep')), may hold values from -6 to 6
Outputs:
- layer_output: bfloat16 [64, 512, 768], P(('fsdp', 'rep'))
- input_grad: float32 [64, 512, 768], P(('fsdp', 'rep'))
- joint_grad: float32 [768, 2304], P('fsdp')
- query_bias_grad: float32 [768], replicated
- value_bias_grad: float32 [768], replicated
- close_grad: float32 [768, 768], P('fsdp')
- close_bias_grad: float32 [768], replicated
- first_gain_grad: float32 [768], replicated
- first_shift_grad: float32 [768], replicated
- expand_grad: float32 [768, 3072], P('fsdp')
- expand_bias_grad: float32 [3072], replicated
- shrink_grad: float32 [3072, 768], P('fsdp')
- shrink_bias_grad: float32 [768], replicated
- second_gain_grad: float32 [768], replicated
- second_shift_grad: float32 [768], replicated
Inputs may be any that keep to these rules, and one draw needn't show every extreme that they name: `segment_ids`: along each packed row of 512 positions the document numbers start at 0, never fall and rise by at most one from a position to the next; every position belongs to a document. Some row holds 512 documents of one position.
All inputs are finite; a program needn't handle non-finite values.
Results may differ from a plain program's by a relative error of at most 0.015.
Values may be sent and summed in bfloat16 or wider, within the bound.
No kernel may reach another device: no remote copies, remote signals or barrier semaphores. Data moves between devices by JAX's collectives and lax.ppermute only.
A program may use at most 192 MiB of HBM per device.

v0:
```python
import math
import jax
import jax.numpy as jnp
from jax import lax
from jax.sharding import PartitionSpec as P

HEADS = 12
EPS = 1e-12


def layer_norm(values, gain, shift):
    average = jnp.mean(values, axis=-1, keepdims=True)
    centred = values - average
    variance = jnp.mean(centred * centred, axis=-1, keepdims=True)
    return centred * lax.rsqrt(variance + EPS) * gain + shift


def gelu_exact(values):
    return jax.nn.gelu(values, approximate=False)


def split_heads(packed):
    pos_count = packed.shape[0]
    model_width = packed.shape[1] // 3
    head_size = model_width // HEADS
    queries = packed[:, :model_width].reshape(pos_count, HEADS, head_size)
    keys_part = packed[:, model_width : 2 * model_width].reshape(pos_count, HEADS, head_size)
    values_part = packed[:, 2 * model_width :].reshape(pos_count, HEADS, head_size)
    return (queries, keys_part, values_part, 1.0 / math.sqrt(head_size))


def masked_scores(queries, keys_part, segments, score_scale):
    scores = (
        jnp.einsum("qhd,khd->hqk", queries, keys_part, preferred_element_type=jnp.float32)
        * score_scale
    )
    same_doc = segments[:, None] == segments[None, :]
    return jnp.where(same_doc[None], scores, -jnp.inf)


def attend_row(packed, segments):
    queries, keys_part, values_part, score_scale = split_heads(packed)
    scores = masked_scores(queries, keys_part, segments, score_scale)
    top_score = jnp.max(scores, axis=-1, keepdims=True)
    raised = jnp.exp(scores - top_score)
    denominator = jnp.sum(raised, axis=-1, keepdims=True)
    attn_low = (raised / denominator).astype(jnp.bfloat16)
    context = jnp.einsum("hqk,khd->qhd", attn_low, values_part, preferred_element_type=jnp.float32)
    return (
        context.reshape(packed.shape[0], packed.shape[1] // 3),
        top_score + jnp.log(denominator),
    )


def attend_back(packed, segments, log_total, grad_context):
    pos_count = packed.shape[0]
    model_width = packed.shape[1] // 3
    queries, keys_part, values_part, score_scale = split_heads(packed)
    scores = masked_scores(queries, keys_part, segments, score_scale)
    attn_weights = jnp.exp(scores - log_total)
    grad_heads = grad_context.reshape(pos_count, HEADS, model_width // HEADS)
    grad_attn = jnp.einsum(
        "qhd,khd->hqk", grad_heads, values_part, preferred_element_type=jnp.float32
    )
    inner_sum = jnp.sum(grad_attn * attn_weights, axis=-1, keepdims=True)
    grad_scores = (attn_weights * (grad_attn - inner_sum)).astype(jnp.bfloat16)
    grad_queries = (
        jnp.einsum("hqk,khd->qhd", grad_scores, keys_part, preferred_element_type=jnp.float32)
        * score_scale
    )
    grad_keys = (
        jnp.einsum("hqk,qhd->khd", grad_scores, queries, preferred_element_type=jnp.float32)
        * score_scale
    )
    grad_values = jnp.einsum(
        "hqk,qhd->khd",
        attn_weights.astype(jnp.bfloat16),
        grad_heads,
        preferred_element_type=jnp.float32,
    )
    return jnp.concatenate(
        [
            grad_queries.reshape(pos_count, model_width),
            grad_keys.reshape(pos_count, model_width),
            grad_values.reshape(pos_count, model_width),
        ],
        axis=1,
    )


def body(
    layer_input,
    segment_ids,
    joint_weight,
    query_bias,
    value_bias,
    close_weight,
    close_bias,
    first_gain,
    first_shift,
    expand_weight,
    expand_bias,
    shrink_weight,
    shrink_bias,
    second_gain,
    second_shift,
    cotangent,
):
    row_count, pos_count, model_width = layer_input.shape
    tok_count = row_count * pos_count
    flat_input = layer_input.reshape(tok_count, model_width)
    joint_full, close_full = (
        lax.all_gather(joint_weight, "fsdp", axis=0, tiled=True),
        lax.all_gather(close_weight, "fsdp", axis=0, tiled=True),
    )
    joint_bias = jnp.concatenate([query_bias, jnp.zeros_like(query_bias), value_bias]).astype(
        jnp.float32
    )
    mixed = jnp.dot(flat_input, joint_full, preferred_element_type=jnp.float32) + joint_bias
    joint_low = mixed.astype(jnp.bfloat16).reshape(row_count, pos_count, 3 * model_width)
    context, log_total = lax.map(
        lambda packet: attend_row(packet[0], packet[1]), (joint_low, segment_ids)
    )
    context_low = context.reshape(tok_count, model_width).astype(jnp.bfloat16)
    expand_full, shrink_full = (
        lax.all_gather(expand_weight, "fsdp", axis=0, tiled=True),
        lax.all_gather(shrink_weight, "fsdp", axis=0, tiled=True),
    )
    branch = jnp.dot(
        context_low, close_full, preferred_element_type=jnp.float32
    ) + close_bias.astype(jnp.float32)
    first_sum = flat_input.astype(jnp.float32) + branch
    hidden, first_pull = jax.vjp(
        layer_norm, first_sum, first_gain.astype(jnp.float32), first_shift.astype(jnp.float32)
    )
    hidden_low = hidden.astype(jnp.bfloat16)
    inner = jnp.dot(
        hidden_low, expand_full, preferred_element_type=jnp.float32
    ) + expand_bias.astype(jnp.float32)
    active, gelu_pull = jax.vjp(gelu_exact, inner)
    active_low = active.astype(jnp.bfloat16)
    ffn_out = jnp.dot(
        active_low, shrink_full, preferred_element_type=jnp.float32
    ) + shrink_bias.astype(jnp.float32)
    output, second_pull = jax.vjp(
        layer_norm,
        hidden + ffn_out,
        second_gain.astype(jnp.float32),
        second_shift.astype(jnp.float32),
    )
    layer_output = output.astype(jnp.bfloat16).reshape(row_count, pos_count, model_width)
    expand_back, shrink_back = (
        lax.all_gather(expand_weight, "fsdp", axis=0, tiled=True),
        lax.all_gather(shrink_weight, "fsdp", axis=0, tiled=True),
    )
    grad_second, second_gain_part, second_shift_part = second_pull(
        cotangent.reshape(tok_count, model_width).astype(jnp.float32)
    )
    grad_ffn = grad_second.astype(jnp.bfloat16)
    shrink_term = jnp.einsum("tf,td->fd", active_low, grad_ffn, preferred_element_type=jnp.float32)
    grad_active = jnp.einsum("td,fd->tf", grad_ffn, shrink_back, preferred_element_type=jnp.float32)
    grad_inner = gelu_pull(grad_active)[0].astype(jnp.bfloat16)
    expand_term = jnp.einsum(
        "td,tf->df", hidden_low, grad_inner, preferred_element_type=jnp.float32
    )
    grad_hidden = grad_second + jnp.einsum(
        "tf,df->td", grad_inner, expand_back, preferred_element_type=jnp.float32
    )
    expand_part, shrink_part = (
        lax.psum_scatter(expand_term, "fsdp", scatter_dimension=0, tiled=True),
        lax.psum_scatter(shrink_term, "fsdp", scatter_dimension=0, tiled=True),
    )
    grad_first, first_gain_part, first_shift_part = first_pull(grad_hidden)
    grad_branch = grad_first.astype(jnp.bfloat16)
    joint_back, close_back = (
        lax.all_gather(joint_weight, "fsdp", axis=0, tiled=True),
        lax.all_gather(close_weight, "fsdp", axis=0, tiled=True),
    )
    close_term = jnp.einsum(
        "td,te->de", context_low, grad_branch, preferred_element_type=jnp.float32
    )
    grad_context = jnp.einsum(
        "te,de->td", grad_branch, close_back, preferred_element_type=jnp.float32
    ).astype(jnp.bfloat16)
    grad_mixed = lax.map(
        lambda packet: attend_back(packet[0], packet[1], packet[2], packet[3]),
        (
            joint_low,
            segment_ids,
            log_total,
            grad_context.reshape(row_count, pos_count, model_width),
        ),
    )
    grad_mixed_low = grad_mixed.reshape(tok_count, 3 * model_width).astype(jnp.bfloat16)
    joint_term = jnp.einsum(
        "td,te->de", flat_input, grad_mixed_low, preferred_element_type=jnp.float32
    )
    input_grad = grad_first + jnp.einsum(
        "te,de->td", grad_mixed_low, joint_back, preferred_element_type=jnp.float32
    )
    joint_part, close_part = (
        lax.psum_scatter(joint_term, "fsdp", scatter_dimension=0, tiled=True),
        lax.psum_scatter(close_term, "fsdp", scatter_dimension=0, tiled=True),
    )
    joint_grad, close_grad, expand_grad, shrink_grad = (
        lax.psum(joint_part.astype(jnp.bfloat16), "rep").astype(jnp.float32),
        lax.psum(close_part.astype(jnp.bfloat16), "rep").astype(jnp.float32),
        lax.psum(expand_part.astype(jnp.bfloat16), "rep").astype(jnp.float32),
        lax.psum(shrink_part.astype(jnp.bfloat16), "rep").astype(jnp.float32),
    )
    grad_mixed_wide = grad_mixed_low.astype(jnp.float32)
    vector_terms = (
        jnp.sum(grad_mixed_wide[:, :model_width], axis=0),
        jnp.sum(grad_mixed_wide[:, 2 * model_width :], axis=0),
        jnp.sum(grad_branch.astype(jnp.float32), axis=0),
        first_gain_part,
        first_shift_part,
        jnp.sum(grad_inner.astype(jnp.float32), axis=0),
        jnp.sum(grad_ffn.astype(jnp.float32), axis=0),
        second_gain_part,
        second_shift_part,
    )
    (
        query_bias_grad,
        value_bias_grad,
        close_bias_grad,
        first_gain_grad,
        first_shift_grad,
        expand_bias_grad,
        shrink_bias_grad,
        second_gain_grad,
        second_shift_grad,
    ) = lax.psum(
        (
            vector_terms[0],
            vector_terms[1],
            vector_terms[2],
            vector_terms[3],
            vector_terms[4],
            vector_terms[5],
            vector_terms[6],
            vector_terms[7],
            vector_terms[8],
        ),
        ("fsdp", "rep"),
    )
    return (
        layer_output,
        input_grad.reshape(row_count, pos_count, model_width),
        joint_grad,
        query_bias_grad,
        value_bias_grad,
        close_grad,
        close_bias_grad,
        first_gain_grad,
        first_shift_grad,
        expand_grad,
        expand_bias_grad,
        shrink_grad,
        shrink_bias_grad,
        second_gain_grad,
        second_shift_grad,
    )


def solution(mesh):
    placed = (
        P(("fsdp", "rep"), None, None),
        P(("fsdp", "rep"), None),
        P("fsdp", None),
        P(),
        P(),
        P("fsdp", None),
        P(),
        P(),
        P(),
        P("fsdp", None),
        P(),
        P("fsdp", None),
        P(),
        P(),
        P(),
        P(("fsdp", "rep"), None, None),
    )
    return jax.shard_map(
        body,
        mesh=mesh,
        in_specs=placed,
        out_specs=(
            P(("fsdp", "rep"), None, None),
            P(("fsdp", "rep"), None, None),
            P("fsdp", None),
            P(),
            P(),
            P("fsdp", None),
            P(),
            P(),
            P(),
            P("fsdp", None),
            P(),
            P("fsdp", None),
            P(),
            P(),
            P(),
        ),
        check_vma=False,
    )
```

profile of v0, /device:TPU:0, one launch (start us, length us, event | category | flops | bytes accessed | tf_op | source)
XLA Modules:
  0.0 939.9 jit_solution(8562727655183991149)
XLA Ops:
  19.7 57.8 %all-gather.5.cloned.1.call-done = bf16[768,2304]{1,0:T(8,128)(2,1)} async-done(((bf16[96,2304]{1,0:T(8,128)(2,1)}), bf16[768,2304]{1,0:T(8,128)(2,1)}) %all-gather.5.cloned.1.call-update) | async-done | bytes 3538960 | tf_op jit(solution)/shard_map/all_gather | solution.py:113
  77.5 8.4 add_convert_fusion.1
  86.0 6.8 copy.54
  92.8 23.4 %while.22 = (s32[]{:T(128)}, bf16[2,512,768]{2,1,0:T(8,128)(2,1)}, f32[2,12,512,1]{2,1,3,0:T(8,128)S(1)}, bf16[2,512,2304]{1,2,0:T(8,128)(2,1)}, s32[2,512]{1,0:T(2,128)S(1)}, /*index=5*/s32[]{:T(128)}) while((s32[]{:T(128)}, bf16[2,512,768]{2,1,0:T(8,128)(2,1)}, f32[2,12,512,1]{2,1,3,0:T(8,128)S(1)}, bf16[2,512,2304]{1,2,0:T(8,128)(2,1)}, ...), condition=%wide.region_3.4_spmd, body=%wide.region_0.3_spmd.sunk | while | flops 843311104 | bytes 54753372 | solution.py:121
  97.1 2.5 fusion.97
  99.6 3.6 fusion.98
  106.7 2.1 fusion.96
  108.8 2.5 fusion.97
  111.3 3.6 fusion.98
  116.2 3.4 all-gather.7.cloned.1.call-done
  119.6 3.8 fusion.33
  124.0 75.9 %all-gather.9.cloned.1.call-done = bf16[768,3072]{1,0:T(8,128)(2,1)} async-done(((bf16[96,3072]{1,0:T(8,128)(2,1)}), bf16[768,3072]{1,0:T(8,128)(2,1)}) %all-gather.9.cloned.1.call-update) | async-done | bytes 4718608 | tf_op jit(solution)/shard_map/all_gather | solution.py:126
  199.8 36.0 %multiply_convert_fusion.1 = (bf16[1024,3072]{1,0:T(8,128)(2,1)}, f32[1024,3072]{1,0:T(8,128)}, f32[1024,3072]{1,0:T(8,128)}) fusion(f32[3072]{0:T(1024)S(1)} %copy-done.28, bf16[768,3072]{1,0:T(8,128)(2,1)} %all-gather.9.cloned.1.call-done, f32[1024,768]{1,0:T(8,128)S(1)} %get-tuple-element.220, f32[768]{0:T(1024)S(1)} %copy-done.19, ...), kind=kOutput, calls=%fused_computation.34 | convolution fusion | flops 5043388416 | bytes 39348224 | tf_op jit(solution)/shard_map/dot_general | solution.py:137
  235.8 43.8 %all-gather.11.cloned.1.call-done = bf16[3072,768]{1,0:T(8,128)(2,1)} async-done(((bf16[384,768]{1,0:T(8,128)(2,1)}), bf16[3072,768]{1,0:T(8,128)(2,1)}) %all-gather.11.cloned.1.call-update) | async-done | bytes 4718608 | tf_op jit(solution)/shard_map/all_gather | solution.py:127
  279.6 8.9 fusion.34
  290.9 2.6 fusion.29
  295.5 19.4 %convert_reduce_fusion = (f32[3072]{0:T(1024)}, bf16[1024,3072]{1,0:T(8,128)(2,1)}) fusion(f32[1024,3072]{1,0:T(8,128)} %get-tuple-element.207, bf16[1024,768]{1,0:T(8,128)(2,1)} %get-tuple-element.199, bf16[3072,768]{1,0:T(8,128)(2,1)} %all-gather.11.cloned.1.call-done, f32[1024,3072]{1,0:T(8,128)} %get-tuple-element.221, f32[3072]{0:T(1024)S(1)} %copy-done.28), kind=kOutput, calls=%fused_computation.32 | convolution fusion | flops 4885312512 | bytes 37773312 | tf_op jit(solution)/shard_map/td,fd->tf/dot_general | solution.py:161
  315.0 10.1 %multiply_reduce_fusion.1 = (f32[768]{0:T(1024)}, f32[1024]{0:T(1024)S(1)}, f32[768]{0:T(1024)}, f32[1024,768]{1,0:T(8,128)S(1)}) fusion(f32[1024,768]{1,0:T(8,128)S(1)} %get-tuple-element.220, f32[1024]{0:T(1024)S(1)} %fusion.22, f32[1024]{0:T(1024)S(1)} %broadcast_multiply_fusion.1, f32[768]{0:T(1024)S(1)} %copy-done.15, ...), kind=kOutput, calls=%fused_computation.62 | convolution fusion | flops 4839699456 | bytes 20472832 | tf_op jit(solution)/shard_map/tf,df->td/dot_general | solution.py:166
  329.2 2.8 fusion.36
  332.1 2.7 convolution_convert_fusion
  334.9 62.1 %while.23 = (s32[]{:T(128)}, bf16[2,512,2304]{2,1,0:T(8,128)(2,1)}, bf16[2,512,2304]{1,2,0:T(8,128)(2,1)}, s32[2,512]{1,0:T(2,128)S(1)}, f32[2,12,512,1]{2,1,3,0...) while((s32[]{:T(128)}, bf16[2,512,2304]{2,1,0:T(8,128)(2,1)}, ...), condition=%wide.region_14.15_spmd, body=%wide.region_12.14_spmd.sunk | while | flops 2069358592 | bytes 142784688 | solution.py:185
  339.5 3.2 fusion.111
  342.7 6.9 multiply_reduce_fusion.6
  349.5 7.1 multiply_convert_fusion.3
  359.9 2.6 copy.95
  362.5 3.3 constant_dynamic-update-slice_fusion.5
  370.3 3.2 fusion.111
  373.4 6.9 multiply_reduce_fusion.6
  380.3 7.2 multiply_convert_fusion.3
  390.8 2.6 copy.95
  393.4 3.4 constant_dynamic-update-slice_fusion.5
  397.0 9.7 %convolution_bitcast_fusion = f32[768,2304]{0,1:T(8,128)} fusion(bf16[2,512,2304]{2,1,0:T(8,128)(2,1)} %get-tuple-element.77, bf16[2,512,768]{2,1,0:T(8,128)(2,1)} %param.20), kind=kOutput, calls=%fused_computation.49 | convolution fusion | flops 3623878656 | bytes 13369344 | tf_op jit(solution)/shard_map/td,te->de/dot_general | solution.py:195
  406.7 8.1 copy.66
  416.6 10.7 %fusion.24 = f32[768,3072]{1,0:T(8,128)} fusion(bf16[1024,3072]{1,0:T(8,128)(2,1)} %get-tuple-element.226, f32[1024,768]{1,0:T(8,128)S(1)} %copy-done.1, f32[768]{0:T(1024)S(1)} %copy-done.20, f32[768]{0:T(1024)S(1)} %copy-done.16, f32[1024]{0:T(1024)S(1)} %copy-done.14, f32[1024]{0:T(1024)S(1)} %copy-done.12), kind=kOutput, calls=%fused_computation.89 | convolution fusion | flops 4835770368 | bytes 18888704 | tf_op jit(solution)/shard_map/td,tf->df/dot_general | solution.py:163
  428.7 10.2 %fusion.37 = f32[3072,768]{1,0:T(8,128)} fusion(bf16[1024,3072]{1,0:T(8,128)(2,1)} %get-tuple-element.206, bf16[1024,768]{1,0:T(8,128)(2,1)S(1)} %copy-done.8), kind=kOutput, calls=%fused_computation.99 | convolution fusion | flops 4831838208 | bytes 17301504 | tf_op jit(solution)/shard_map/tf,td->fd/dot_general | solution.py:160
  440.6 3.1 bitcast_convert_fusion
  444.5 43.5 %all-reduce = (f32[768]{0:T(1024)}, f32[768]{0:T(1024)}, f32[768]{0:T(1024)}, f32[768]{0:T(1024)}, f32[768]{0:T(1024)}, /*index=5*/f32[3072]{0:T(1024)}, f32[768]{0:T(1024)}, f32[768]{0:T(1024)}, f32[768]{0:T(1024)}) all-reduce(f32[768]{0:T(1024)S(1)} %get-tuple-element.157, ...), channel_id=1, replica_groups=mesh['fsdp'=8,'rep'=4] {'fsdp','rep'}, use_global_device_ids=true, to_apply=%region_18.19 | all-reduce | flops 9216 | bytes 73728 | tf_op jit(solution)/shard_map/psum | solution.py:233
  489.6 54.0 %reduce-scatter.13.cloned.1.call-done = f32[96,2304]{1,0:T(8,128)} async-done(((f32[768,2304]{1,0:T(8,128)}), f32[96,2304]{1,0:T(8,128)}) %reduce-scatter.13.cloned.1.call-update) | async-done | bytes 884752
  543.6 2.2 copy.67
  545.9 162.6 %reduce-scatter.9.cloned.1.call-done = f32[96,3072]{1,0:T(8,128)} async-done(((f32[768,3072]{1,0:T(8,128)}), f32[96,3072]{1,0:T(8,128)}) %reduce-scatter.9.cloned.1.call-update) | async-done | bytes 1179664 | tf_op jit(solution)/shard_map/reduce_scatter | solution.py:170
  708.5 2.2 convert_element_type.151
  710.6 162.7 %reduce-scatter.11.cloned.1.call-done = f32[384,768]{1,0:T(8,128)} async-done(((f32[3072,768]{1,0:T(8,128)}), f32[384,768]{1,0:T(8,128)}) %reduce-scatter.11.cloned.1.call-update) | async-done | bytes 1179664 | tf_op jit(solution)/shard_map/reduce_scatter | solution.py:171
  873.3 2.1 convert_element_type.154
  875.5 8.9 add_add_fusion.4
  884.5 40.4 %all-reduce.4.cloned.1.call-done = (bf16[96,2304]{0,1:T(8,128)(2,1)}, bf16[96,768]{1,0:T(8,128)(2,1)}, bf16[96,3072]{1,0:T(8,128)(2,1)}, bf16[384,768]{1,0:T(8,128)(2,1)}) async-done(((bf16[96,2304]{0,1:T(8,128)(2,1)}, bf16[96,768]{1,0:T(8,128)(2,1)}, bf16[96,3072]{1,0:T(8,128)(2,1)}, bf16[384,768]{1,0:T(8,128)(2,1)}), (bf16[96,2304]{0,1:T(8,128)(2,1)}, bf16[96,768]{1,0:T(8,128)(2,1)}, ...) | async-done | bytes 1769488 | tf_op jit(solution)/shard_map/psum | solution.py:206
  924.9 2.2 copy.60
  928.7 2.2 convert_element_type.152
  930.9 2.2 convert_element_type.155
  (160 shorter events, 54.7 us)
Async XLA Ops:
  7.2 70.3 %all-gather.5.cloned.1.call-start = ((), (), s32[]{:S(2)}) async-start(), calls=%async_computation.4 | async-start | bytes 3981312 | tf_op jit(solution)/shard_map/all_gather | solution.py:113
  7.9 111.7 %all-gather.7.cloned.1.call-start = ((), (), s32[]{:S(2)}) async-start(), calls=%async_computation.5 | async-start | bytes 1327104 | tf_op jit(solution)/shard_map/all_gather | solution.py:114
  8.7 191.2 %all-gather.9.cloned.1.call-start = ((), (), s32[]{:S(2)}) async-start(), calls=%async_computation.6 | async-start | bytes 5308416 | tf_op jit(solution)/shard_map/all_gather | solution.py:126
  9.4 270.2 %all-gather.11.cloned.1.call-start = ((), (), s32[]{:S(2)}) async-start(), calls=%async_computation.7 | async-start | bytes 5308416 | tf_op jit(solution)/shard_map/all_gather | solution.py:127
  10.0 478.0 %reduce-scatter.7.cloned.1.call-start = ((), (), s32[]{:S(2)}) async-start(), calls=%async_computation.8 | async-start | bytes 2654208 | tf_op jit(solution)/shard_map/reduce_scatter | solution.py:203
  86.0 6.8 copy-start.17
  92.8 26.8 %copy-start.31 = (f32[768]{0:T(1024)S(1)}, f32[768]{0:T(1024)}, u32[]{:S(2)}) copy-start(f32[768]{0:T(1024)} %convert_element_type.127) | copy-start | bytes 9220
  116.2 3.4 copy-start.9
  119.6 80.2 %copy-start.15 = (f32[768]{0:T(1024)S(1)}, f32[768]{0:T(1024)}, u32[]{:S(2)}) copy-start(f32[768]{0:T(1024)} %convert_element_type.128) | copy-start | bytes 9220
  119.6 80.2 %copy-start.19 = (f32[768]{0:T(1024)S(1)}, f32[768]{0:T(1024)}, u32[]{:S(2)}) copy-start(f32[768]{0:T(1024)} %convert_element_type.129) | copy-start | bytes 9220
  119.6 80.2 %copy-start.28 = (f32[3072]{0:T(1024)S(1)}, f32[3072]{0:T(1024)}, u32[]{:S(2)}) copy-start(f32[3072]{0:T(1024)} %convert_element_type.131) | copy-start | bytes 36868
  123.4 201.7 %copy-start = (f32[1024,768]{1,0:T(8,128)}, f32[1024,768]{1,0:T(8,128)S(1)}, u32[]{:S(2)}) copy-start(f32[1024,768]{1,0:T(8,128)S(1)} %get-tuple-element.220) | copy-start | bytes 9437188
  123.4 201.7 %copy-start.11 = (f32[1024]{0:T(1024)}, f32[1024]{0:T(1024)S(1)}, u32[]{:S(2)}) copy-start(f32[1024]{0:T(1024)S(1)} %broadcast_multiply_fusion.1) | copy-start | bytes 12292
  123.9 201.2 %copy-start.13 = (f32[1024]{0:T(1024)}, f32[1024]{0:T(1024)S(1)}, u32[]{:S(2)}) copy-start(f32[1024]{0:T(1024)S(1)} %fusion.22) | copy-start | bytes 12292
  123.9 155.6 %copy-start.30 = (f32[768]{0:T(1024)S(1)}, f32[768]{0:T(1024)}, u32[]{:S(2)}) copy-start(f32[768]{0:T(1024)} %convert_element_type.133) | copy-start | bytes 9220
  279.6 9.5 %copy-start.2 = (bf16[2,512,768]{2,1,0:T(8,128)(2,1)S(1)}, bf16[2,512,768]{2,1,0:T(8,128)(2,1)}, u32[]{:S(2)}) copy-start(bf16[2,512,768]{2,1,0:T(8,128)(2,1)} %param.35) | copy-start | bytes 4718596
  279.6 9.5 %copy-start.21 = (f32[768]{0:T(1024)S(1)}, f32[768]{0:T(1024)}, u32[]{:S(2)}) copy-start(f32[768]{0:T(1024)} %convert_element_type.134) | copy-start | bytes 9220
  288.5 2.3 copy-start.24
  326.6 1.7 copy-start.4
  326.6 2.6 copy-start.34
  326.6 2.6 copy-start.22
  332.1 2.8 copy-start.10
  332.1 2.8 copy-start.18
  332.1 211.5 %reduce-scatter.13.cloned.1.call-start = ((), (), s32[]{:S(2)}) async-start(), calls=%async_computation.11 | async-start | bytes 7962624
  335.0 2.6 copy-start.6
  362.5 3.3 copy-start.7
  365.8 2.6 copy-start.6
  393.3 3.4 copy-start.7
  414.7 1.9 copy-start.1
  414.7 1.9 copy-start.12
  414.7 1.9 copy-start.14
  414.7 1.9 copy-start.16
  414.7 1.9 copy-start.20
  414.8 293.7 %reduce-scatter.9.cloned.1.call-start = ((), (), s32[]{:S(2)}) async-start(), calls=%async_computation.9 | async-start | bytes 10616832 | tf_op jit(solution)/shard_map/reduce_scatter | solution.py:170
  427.3 1.4 copy-start.8
  427.3 446.0 %reduce-scatter.11.cloned.1.call-start = ((), (), s32[]{:S(2)}) async-start(), calls=%async_computation.10 | async-start | bytes 10616832 | tf_op jit(solution)/shard_map/reduce_scatter | solution.py:171
  438.9 1.4 copy-start.3
  438.9 485.9 %all-reduce.4.cloned.1.call-start = ((), (), s32[]{:S(2)}) async-start(), calls=%async_computation.12 | async-start | bytes 3833856 | tf_op jit(solution)/shard_map/psum | solution.py:206
  443.7 0.7 copy-start.25
  443.8 0.7 copy-start.26
  443.8 0.7 copy-start.27
  443.8 0.7 copy-start.29
  443.8 0.7 copy-start.32
  443.8 0.7 copy-start.33
  444.2 431.3 %copy-start.5 = (f32[1024,768]{1,0:T(8,128)S(1)}, f32[1024,768]{1,0:T(8,128)}, u32[]{:S(2)}) copy-start(f32[1024,768]{1,0:T(8,128)} %copy-done.4) | copy-start | bytes 9437188
  444.2 431.3 %copy-start.23 = (f32[1024]{0:T(1024)S(1)}, f32[1024]{0:T(1024)}, u32[]{:S(2)}) copy-start(f32[1024]{0:T(1024)} %copy-done.22) | copy-start | bytes 12292
Sparse Core Ops, SparseCore 0:
  10.2 67.3 all-gather.4
  79.7 39.8 all-gather.6
  121.8 78.0 all-gather.8
  201.9 77.6 all-gather.10
  332.2 67.9 reduce-scatter.6
  414.9 128.6 reduce-scatter.12
  547.2 161.2 reduce-scatter.8
  712.1 161.1 reduce-scatter.10
  877.1 47.7 all-reduce.3
where the time goes:
time: 944 us; the launch traced here: 940 us
  waiting for transfers between devices  603 us (64%)
  matrix products  173 us (18%)
  other arithmetic  55.7 us (6%)
  local copies, waits for them, and re-layouts  48.9 us (5%)
  blocking collectives  43.5 us (5%)
  between operations  14.5 us (2%)
    reduce_scatter x1, waiting for transfers between devices, body(): lax.psum_scatter(shrink_term, 'fsdp', scatter_dimension=0, tiled=True)  163 us
    reduce_scatter x1, waiting for transfers between devices, body(): lax.psum_scatter(expand_term, 'fsdp', scatter_dimension=0, tiled=True)  163 us
    all_gather x1, waiting for transfers between devices, body(): lax.all_gather(expand_weight, 'fsdp', axis=0, tiled=True)  75.9 us
    all_gather x1, waiting for transfers between devices, body(): lax.all_gather(joint_weight, 'fsdp', axis=0, tiled=True)  57.8 us
    unnamed x10, waiting for transfers between devices  56.7 us
    all_gather x1, waiting for transfers between devices, body(): lax.all_gather(shrink_weight, 'fsdp', axis=0, tiled=True)  43.8 us
    psum x1, blocking collectives, body(): lax.psum((vector_terms[0], vector_terms[1], vector_terms[2], vector_terms...  43.5 us
    psum x1, waiting for transfers between devices, body(): lax.psum(joint_part.astype(jnp.bfloat16), 'rep').astype(jnp.float32)  40.4 us
  transfers between devices with their start and end apart: 9, of which 8 were waited for; matrix products, arithmetic and copies ran while one was open for 22% of the time, Pallas kernels for 0%

commit v1 on v0

--- a/solution.py
+++ b/solution.py
@@ -202,8 +202,12 @@
         lax.psum_scatter(joint_term, "fsdp", scatter_dimension=0, tiled=True),
         lax.psum_scatter(close_term, "fsdp", scatter_dimension=0, tiled=True),
     )
+
+    def prepare_spot(w_in):
+        return jnp.sum(lax.all_gather(w_in, axis_name="rep"), axis=0)
+
     joint_grad, close_grad, expand_grad, shrink_grad = (
-        lax.psum(joint_part.astype(jnp.bfloat16), "rep").astype(jnp.float32),
+        prepare_spot(joint_part.astype(jnp.bfloat16)).astype(jnp.float32),
         lax.psum(close_part.astype(jnp.bfloat16), "rep").astype(jnp.float32),
         lax.psum(expand_part.astype(jnp.bfloat16), "rep").astype(jnp.float32),
         lax.psum(shrink_part.astype(jnp.bfloat16), "rep").astype(jnp.float32),

time: 944 us -> 1050 us (1.11)
  waiting for transfers between devices: 603 us -> 686 us
  matrix products: 173 us -> 192 us
    reduce_scatter x0 -> x1, waiting for transfers between devices: none -> 99.9 us  [body(): lax.psum_scatter(joint_term, 'fsdp', scatter_dimension=0, tiled=True)]
    unnamed x10, waiting for transfers between devices: 56.7 us -> 2.68 us
    reduce_scatter x1, waiting for transfers between devices: 0.01 us -> 25.2 us  [body(): lax.psum_scatter(close_term, 'fsdp', scatter_dimension=0, tiled=True)]
    all_gather x0 -> x1, waiting for transfers between devices: none -> 10.9 us  [prepare_spot(): return jnp.sum(lax.all_gather(w_in, axis_name='rep'), axis=0)]
  transfers between devices with their start and end apart: 9 -> 10, of which waited for: 8 -> 10; matrix products, arithmetic and copies ran while one was open for 22% -> 13% of each run, Pallas kernels for 0% -> 0%
where the time goes in v1:
time: 1050 us; the launch traced here: 1040 us
  waiting for transfers between devices  686 us (65%)
  matrix products  192 us (18%)
  other arithmetic  60 us (6%)
  local copies, waits for them, and re-layouts  47.9 us (5%)
  blocking collectives  41.3 us (4%)
  between operations  14.9 us (1%)
    reduce_scatter x1, waiting for transfers between devices, body(): lax.psum_scatter(expand_term, 'fsdp', scatter_dimension=0, tiled=True)  163 us
    reduce_scatter x1, waiting for transfers between devices, body(): lax.psum_scatter(shrink_term, 'fsdp', scatter_dimension=0, tiled=True)  163 us
    reduce_scatter x1, waiting for transfers between devices, body(): lax.psum_scatter(joint_term, 'fsdp', scatter_dimension=0, tiled=True)  99.9 us
    all_gather x1, waiting for transfers between devices, body(): lax.all_gather(expand_weight, 'fsdp', axis=0, tiled=True)  75.9 us
    all_gather x1, waiting for transfers between devices, body(): lax.all_gather(joint_weight, 'fsdp', axis=0, tiled=True)  57.8 us
    all_gather x1, waiting for transfers between devices, body(): lax.all_gather(shrink_weight, 'fsdp', axis=0, tiled=True)  43.7 us
    psum x1, blocking collectives, body(): lax.psum((vector_terms[0], vector_terms[1], vector_terms[2], vector_terms...  41.3 us
    psum x1, waiting for transfers between devices, body(): lax.psum(close_part.astype(jnp.bfloat16), 'rep').astype(jnp.float32)  40.4 us
  transfers between devices with their start and end apart: 10, of which 10 were waited for; matrix products, arithmetic and copies ran while one was open for 13% of the time, Pallas kernels for 0%

profile of v1, /device:TPU:0, one launch (start us, length us, event | category | flops | bytes accessed | tf_op | source)
XLA Modules:
  0.0 1043.6 jit_solution(5206604371495511188)
XLA Ops:
  19.7 57.8 %all-gather.7.cloned.1.call-done = bf16[768,2304]{1,0:T(8,128)(2,1)} async-done(((bf16[96,2304]{1,0:T(8,128)(2,1)}), bf16[768,2304]{1,0:T(8,128)(2,1)}) %all-gather.7.cloned.1.call-update) | async-done | bytes 3538960 | tf_op jit(solution)/shard_map/all_gather | solution.py:113
  77.5 8.5 add_convert_fusion.1
  86.1 6.9 copy.64
  93.0 23.5 %while.22 = (s32[]{:T(128)}, bf16[2,512,768]{2,1,0:T(8,128)(2,1)}, f32[2,12,512,1]{2,1,3,0:T(8,128)S(1)}, bf16[2,512,2304]{1,2,0:T(8,128)(2,1)}, s32[2,512]{1,0:T(2,128)S(1)}, /*index=5*/s32[]{:T(128)}) while((s32[]{:T(128)}, bf16[2,512,768]{2,1,0:T(8,128)(2,1)}, f32[2,12,512,1]{2,1,3,0:T(8,128)S(1)}, bf16[2,512,2304]{1,2,0:T(8,128)(2,1)}, ...), condition=%wide.region_3.4_spmd, body=%wide.region_0.3_spmd.sunk | while | flops 843311104 | bytes 54753872 | solution.py:121
  97.3 2.5 fusion.97
  99.9 3.6 fusion.98
  109.0 2.5 fusion.97
  111.6 3.6 fusion.98
  116.4 3.2 all-gather.9.cloned.1.call-done
  119.6 3.8 fusion.33
  124.0 75.9 %all-gather.11.cloned.1.call-done = bf16[768,3072]{1,0:T(8,128)(2,1)} async-done(((bf16[96,3072]{1,0:T(8,128)(2,1)}), bf16[768,3072]{1,0:T(8,128)(2,1)}) %all-gather.11.cloned.1.call-update) | async-done | bytes 4718608 | tf_op jit(solution)/shard_map/all_gather | solution.py:126
  199.8 36.1 %multiply_convert_fusion.1 = (bf16[1024,3072]{1,0:T(8,128)(2,1)}, f32[1024,3072]{1,0:T(8,128)}, f32[1024,3072]{1,0:T(8,128)}) fusion(f32[3072]{0:T(1024)S(1)} %copy-done.28, bf16[768,3072]{1,0:T(8,128)(2,1)} %all-gather.11.cloned.1.call-done, f32[1024,768]{1,0:T(8,128)S(1)} %get-tuple-element.185, f32[768]{0:T(1024)S(1)} %copy-done.19, ...), kind=kOutput, calls=%fused_computation.34 | convolution fusion | flops 5043388416 | bytes 39348224 | tf_op jit(solution)/shard_map/dot_general | solution.py:137
  235.9 43.7 %all-gather.13.cloned.1.call-done = bf16[3072,768]{1,0:T(8,128)(2,1)} async-done(((bf16[384,768]{1,0:T(8,128)(2,1)}), bf16[3072,768]{1,0:T(8,128)(2,1)}) %all-gather.13.cloned.1.call-update) | async-done | bytes 4718608 | tf_op jit(solution)/shard_map/all_gather | solution.py:127
  279.6 8.9 fusion.34
  290.9 2.6 fusion.29
  295.5 19.1 %convert_reduce_fusion = (f32[3072]{0:T(1024)}, bf16[1024,3072]{1,0:T(8,128)(2,1)}) fusion(f32[1024,3072]{1,0:T(8,128)} %get-tuple-element.172, bf16[1024,768]{1,0:T(8,128)(2,1)} %get-tuple-element.164, bf16[3072,768]{1,0:T(8,128)(2,1)} %all-gather.13.cloned.1.call-done, f32[1024,3072]{1,0:T(8,128)} %get-tuple-element.186, f32[3072]{0:T(1024)S(1)} %copy-done.28), kind=kOutput, calls=%fused_computation.32 | convolution fusion | flops 4885312512 | bytes 37773312 | tf_op jit(solution)/shard_map/td,fd->tf/dot_general | solution.py:161
  314.7 10.1 multiply_reduce_fusion.1
  328.4 2.6 convolution_convert_fusion
  331.1 86.2 %while.23 = (s32[]{:T(128)}, bf16[2,512,2304]{2,1,0:T(8,128)(2,1)}, bf16[2,512,2304]{1,2,0:T(8,128)(2,1)}, s32[2,512]{1,0:T(2,128)S(1)}, f32[2,12,512,1]{2,1,3,0...) while((s32[]{:T(128)}, bf16[2,512,2304]{2,1,0:T(8,128)(2,1)}, bf16[2,512,2304]{1,2,0:T(8,128)(2,1)}, ...), condition=%wide.region_14.15_spmd, body=%wide.region_12.14_spmd.sunk | while | flops 2069358592 | bytes 174242512 | solution.py:185
  333.3 6.4 fusion.110
  342.3 11.0 %multiply_reduce_fusion.6 = (f32[12,512]{1,0:T(8,128)S(1)}, f32[12,512,512]{1,2,0:T(8,128)}) fusion(f32[12,512,512]{1,2,0:T(8,128)} %fusion.110, f32[12,512]{1,0:T(8,128)S(1)} %dynamic-slice_bitcast_fusion.8, pred[512,512]{0,1:T(8,128)(4,1)S(1)} %broadcast_compare_fusion.5, bf16[512,12,64]{0,2,1:T(8,128)(2,1)S(1)} %bitcast.163, ...), kind=kOutput, calls=%fused_computation.14.clone.1 | convolution fusion | flops 418375680 | bytes 27049984 | tf_op jit(solution)/shard_map/while/body/eval_jaxpr/qhd,khd->hqk/dot_general | solution.py:62
  354.9 7.0 multiply_convert_fusion.3
  365.1 3.2 fusion.111
  368.4 2.5 copy.105
  370.9 3.2 constant_dynamic-update-slice_fusion.5
  376.2 6.4 fusion.110
  385.2 11.0 %multiply_reduce_fusion.6 = (f32[12,512]{1,0:T(8,128)S(1)}, f32[12,512,512]{1,2,0:T(8,128)}) fusion(f32[12,512,512]{1,2,0:T(8,128)} %fusion.110, f32[12,512]{1,0:T(8,128)S(1)} %dynamic-slice_bitcast_fusion.8, pred[512,512]{0,1:T(8,128)(4,1)S(1)} %broadcast_compare_fusion.5, bf16[512,12,64]{0,2,1:T(8,128)(2,1)S(1)} %bitcast.163, ...), kind=kOutput, calls=%fused_computation.14.clone.1 | convolution fusion | flops 418375680 | bytes 27049984 | tf_op jit(solution)/shard_map/while/body/eval_jaxpr/qhd,khd->hqk/dot_general | solution.py:62
  397.8 7.0 multiply_convert_fusion.3
  408.0 3.2 fusion.111
  411.3 2.5 copy.105
  413.8 3.2 constant_dynamic-update-slice_fusion.5
  417.2 9.7 convolution_bitcast_fusion
  426.9 8.0 copy.76
  435.1 4.9 fusion.36
  440.1 10.9 %fusion.24 = f32[768,3072]{1,0:T(8,128)} fusion(bf16[1024,3072]{1,0:T(8,128)(2,1)} %get-tuple-element.191, f32[1024,768]{1,0:T(8,128)S(1)} %copy-done.1, f32[768]{0:T(1024)S(1)} %copy-done.20, f32[768]{0:T(1024)S(1)} %copy-done.16, f32[1024]{0:T(1024)S(1)} %copy-done.14, f32[1024]{0:T(1024)S(1)} %copy-done.12), kind=kOutput, calls=%fused_computation.89 | convolution fusion | flops 4835770368 | bytes 18888704 | tf_op jit(solution)/shard_map/td,tf->df/dot_general | solution.py:163
  452.4 10.2 fusion.37
  462.7 99.9 %reduce-scatter.13.cloned.1.call-done = f32[96,2304]{1,0:T(8,128)} async-done(((f32[768,2304]{1,0:T(8,128)}), f32[96,2304]{1,0:T(8,128)}) %reduce-scatter.13.cloned.1.call-update) | async-done | bytes 884752 | tf_op jit(solution)/shard_map/reduce_scatter | solution.py:202
  565.2 3.0 bitcast_convert_fusion
  569.0 41.3 %all-reduce = (f32[768]{0:T(1024)}, f32[768]{0:T(1024)}, f32[768]{0:T(1024)}, f32[768]{0:T(1024)}, f32[768]{0:T(1024)}, /*index=5*/f32[3072]{0:T(1024)}, f32[768]{0:T(1024)}, f32[768]{0:T(1024)}, f32[768]{0:T(1024)}) all-reduce(f32[768]{0:T(1024)S(1)} %get-tuple-element.123, ...), channel_id=1, replica_groups=mesh['fsdp'=8,'rep'=4] {'fsdp','rep'}, use_global_device_ids=true, to_apply=%region_18.19 | all-reduce | flops 9216 | bytes 73728 | tf_op jit(solution)/shard_map/psum | solution.py:237
  610.3 25.2 %reduce-scatter.7.cloned.1.call-done = f32[96,768]{1,0:T(8,128)} async-done(((f32[768,768]{1,0:T(8,128)}), f32[96,768]{1,0:T(8,128)}) %reduce-scatter.7.cloned.1.call-update) | async-done | bytes 294928 | tf_op jit(solution)/shard_map/reduce_scatter | solution.py:203
  637.2 163.3 %reduce-scatter.9.cloned.1.call-done = f32[96,3072]{1,0:T(8,128)} async-done(((f32[768,3072]{1,0:T(8,128)}), f32[96,3072]{1,0:T(8,128)}) %reduce-scatter.9.cloned.1.call-update) | async-done | bytes 1179664 | tf_op jit(solution)/shard_map/reduce_scatter | solution.py:170
  800.5 2.2 convert_element_type.153
  802.7 162.7 %reduce-scatter.11.cloned.1.call-done = f32[384,768]{1,0:T(8,128)} async-done(((f32[3072,768]{1,0:T(8,128)}), f32[384,768]{1,0:T(8,128)}) %reduce-scatter.11.cloned.1.call-update) | async-done | bytes 1179664 | tf_op jit(solution)/shard_map/reduce_scatter | solution.py:171
  967.5 9.0 add_add_fusion.4
  976.5 10.9 %all-gather.15.cloned.1.call-done = bf16[384,2304]{1,0:T(8,128)(2,1)} async-done(((bf16[96,2304]{1,0:T(8,128)(2,1)}), bf16[384,2304]{1,0:T(8,128)(2,1)}) %all-gather.15.cloned.1.call-update) | async-done | bytes 1769488 | tf_op jit(solution)/shard_map/all_gather | solution.py:207
  990.1 40.4 %all-reduce.4.cloned.1.call-done = (bf16[96,768]{1,0:T(8,128)(2,1)}, bf16[96,3072]{1,0:T(8,128)(2,1)}, bf16[384,768]{1,0:T(8,128)(2,1)}) async-done(((bf16[96,768]{1,0:T(8,128)(2,1)}, bf16[96,3072]{1,0:T(8,128)(2,1)}, bf16[384,768]{1,0:T(8,128)(2,1)}), (bf16[96,768]{1,0:T(8,128)(2,1)}, bf16[96,3072]{1,0:T(8,128)(2,1)}, bf16[384,768]{1,0:T(8,128)(2,1)})) %all-reduce.4.cloned.1.call-update) | async-done | bytes 1327120 | tf_op jit(solution)/shard_map/psum | solution.py:211
  1030.5 2.2 convert_element_type.154
  1032.7 2.2 convert_element_type.157
  (176 shorter events, 64.1 us)
Async XLA Ops:
  7.2 70.3 %all-gather.7.cloned.1.call-start = ((), (), s32[]{:S(2)}) async-start(), calls=%async_computation.4 | async-start | bytes 3981312 | tf_op jit(solution)/shard_map/all_gather | solution.py:113
  7.9 111.7 %all-gather.9.cloned.1.call-start = ((), (), s32[]{:S(2)}) async-start(), calls=%async_computation.5 | async-start | bytes 1327104 | tf_op jit(solution)/shard_map/all_gather | solution.py:114
  8.7 191.2 %all-gather.11.cloned.1.call-start = ((), (), s32[]{:S(2)}) async-start(), calls=%async_computation.6 | async-start | bytes 5308416 | tf_op jit(solution)/shard_map/all_gather | solution.py:126
  9.4 270.2 %all-gather.13.cloned.1.call-start = ((), (), s32[]{:S(2)}) async-start(), calls=%async_computation.7 | async-start | bytes 5308416 | tf_op jit(solution)/shard_map/all_gather | solution.py:127
  10.0 552.6 %reduce-scatter.13.cloned.1.call-start = ((), (), s32[]{:S(2)}) async-start(), calls=%async_computation.12 | async-start | bytes 7962624 | tf_op jit(solution)/shard_map/reduce_scatter | solution.py:202
  86.1 6.9 copy-start.17
  93.0 26.6 %copy-start.31 = (f32[768]{0:T(1024)S(1)}, f32[768]{0:T(1024)}, u32[]{:S(2)}) copy-start(f32[768]{0:T(1024)} %convert_element_type.129) | copy-start | bytes 9220
  116.4 3.2 copy-start.9
  119.6 80.2 %copy-start.15 = (f32[768]{0:T(1024)S(1)}, f32[768]{0:T(1024)}, u32[]{:S(2)}) copy-start(f32[768]{0:T(1024)} %convert_element_type.130) | copy-start | bytes 9220
  119.6 80.2 %copy-start.19 = (f32[768]{0:T(1024)S(1)}, f32[768]{0:T(1024)}, u32[]{:S(2)}) copy-start(f32[768]{0:T(1024)} %convert_element_type.131) | copy-start | bytes 9220
  119.6 80.2 %copy-start.28 = (f32[3072]{0:T(1024)S(1)}, f32[3072]{0:T(1024)}, u32[]{:S(2)}) copy-start(f32[3072]{0:T(1024)} %convert_element_type.133) | copy-start | bytes 36868
  123.4 201.4 %copy-start = (f32[1024,768]{1,0:T(8,128)}, f32[1024,768]{1,0:T(8,128)S(1)}, u32[]{:S(2)}) copy-start(f32[1024,768]{1,0:T(8,128)S(1)} %get-tuple-element.185) | copy-start | bytes 9437188
  123.4 201.4 %copy-start.11 = (f32[1024]{0:T(1024)}, f32[1024]{0:T(1024)S(1)}, u32[]{:S(2)}) copy-start(f32[1024]{0:T(1024)S(1)} %broadcast_multiply_fusion.1) | copy-start | bytes 12292
  123.9 200.9 %copy-start.13 = (f32[1024]{0:T(1024)}, f32[1024]{0:T(1024)S(1)}, u32[]{:S(2)}) copy-start(f32[1024]{0:T(1024)S(1)} %fusion.22) | copy-start | bytes 12292
  123.9 155.6 %copy-start.30 = (f32[768]{0:T(1024)S(1)}, f32[768]{0:T(1024)}, u32[]{:S(2)}) copy-start(f32[768]{0:T(1024)} %convert_element_type.135) | copy-start | bytes 9220
  279.6 9.5 copy-start.2
  279.6 9.5 copy-start.21
  288.5 2.3 copy-start.24
  326.3 4.8 copy-start.4
  326.3 2.1 copy-start.34
  326.3 4.7 copy-start.22
  327.3 3.8 copy-start.8
  328.4 2.6 copy-start.10
  328.4 2.6 copy-start.18
  333.3 6.7 copy-start.6
  342.3 11.0 %slice-start = ((s8[12582912]{0:T(1024)(128)(4,1)}), s8[4194304]{0:T(1024)(128)(4,1)S(1)}, s32[]{:S(2)}) async-start(s8[12582912]{0:T(1024)(128)(4,1)} %bitcast.153), calls=%async_computation.14 | async-start | bytes 8388608 | tf_op jit(solution)/shard_map/while
  342.3 11.0 %slice-start.1 = ((s8[12582912]{0:T(1024)(128)(4,1)}), s8[4194304]{0:T(1024)(128)(4,1)S(1)}, s32[]{:S(2)}) async-start(s8[12582912]{0:T(1024)(128)(4,1)} %bitcast.153), calls=%async_computation.15 | async-start | bytes 8388608 | tf_op jit(solution)/shard_map/while
  342.3 12.6 %slice-start.2 = ((s8[12582912]{0:T(1024)(128)(4,1)}), s8[4194304]{0:T(1024)(128)(4,1)S(1)}, s32[]{:S(2)}) async-start(s8[12582912]{0:T(1024)(128)(4,1)} %bitcast.153), calls=%async_computation.16 | async-start | bytes 8388608 | tf_op jit(solution)/shard_map/while
  376.1 6.7 copy-start.6
  385.2 11.0 %slice-start = ((s8[12582912]{0:T(1024)(128)(4,1)}), s8[4194304]{0:T(1024)(128)(4,1)S(1)}, s32[]{:S(2)}) async-start(s8[12582912]{0:T(1024)(128)(4,1)} %bitcast.153), calls=%async_computation.14 | async-start | bytes 8388608 | tf_op jit(solution)/shard_map/while
  385.2 11.0 %slice-start.1 = ((s8[12582912]{0:T(1024)(128)(4,1)}), s8[4194304]{0:T(1024)(128)(4,1)S(1)}, s32[]{:S(2)}) async-start(s8[12582912]{0:T(1024)(128)(4,1)} %bitcast.153), calls=%async_computation.15 | async-start | bytes 8388608 | tf_op jit(solution)/shard_map/while
  385.2 12.6 %slice-start.2 = ((s8[12582912]{0:T(1024)(128)(4,1)}), s8[4194304]{0:T(1024)(128)(4,1)S(1)}, s32[]{:S(2)}) async-start(s8[12582912]{0:T(1024)(128)(4,1)} %bitcast.153), calls=%async_computation.16 | async-start | bytes 8388608 | tf_op jit(solution)/shard_map/while
  435.0 5.1 copy-start.1
  435.0 5.1 copy-start.12
  435.0 5.1 copy-start.14
  435.0 5.1 copy-start.16
  435.0 5.1 copy-start.20
  435.0 200.6 %reduce-scatter.7.cloned.1.call-start = ((), (), s32[]{:S(2)}) async-start(), calls=%async_computation.8 | async-start | bytes 2654208 | tf_op jit(solution)/shard_map/reduce_scatter | solution.py:203
  440.0 360.5 %reduce-scatter.9.cloned.1.call-start = ((), (), s32[]{:S(2)}) async-start(), calls=%async_computation.9 | async-start | bytes 10616832 | tf_op jit(solution)/shard_map/reduce_scatter | solution.py:170
  451.0 1.4 copy-start.7
  451.1 514.3 %reduce-scatter.11.cloned.1.call-start = ((), (), s32[]{:S(2)}) async-start(), calls=%async_computation.10 | async-start | bytes 10616832 | tf_op jit(solution)/shard_map/reduce_scatter | solution.py:171
  462.6 102.3 %copy-start.3 = (bf16[2,512,768]{2,1,0:T(8,128)(2,1)S(1)}, bf16[2,512,768]{2,1,0:T(8,128)(2,1)}, u32[]{:S(2)}) copy-start(bf16[2,512,768]{2,1,0:T(8,128)(2,1)} %param.35) | copy-start | bytes 4718596
  462.7 524.7 %all-gather.15.cloned.1.call-start = ((), (), s32[]{:S(2)}) async-start(), calls=%async_computation.11 | async-start | bytes 2211840 | tf_op jit(solution)/shard_map/all_gather | solution.py:207
  564.6 465.9 %all-reduce.4.cloned.1.call-start = ((), (), s32[]{:S(2)}) async-start(), calls=%async_computation.13 | async-start | bytes 2654208 | tf_op jit(solution)/shard_map/psum | solution.py:211
  568.3 0.7 copy-start.29
  568.3 0.7 copy-start.32
  568.3 399.2 %copy-start.5 = (f32[1024,768]{1,0:T(8,128)S(1)}, f32[1024,768]{1,0:T(8,128)}, u32[]{:S(2)}) copy-start(f32[1024,768]{1,0:T(8,128)} %copy-done.4) | copy-start | bytes 9437188
  568.3 399.2 %copy-start.23 = (f32[1024]{0:T(1024)S(1)}, f32[1024]{0:T(1024)}, u32[]{:S(2)}) copy-start(f32[1024]{0:T(1024)} %copy-done.22) | copy-start | bytes 12292
  (4 other events, 2.8 us)
Sparse Core Ops, SparseCore 0:
  10.2 67.3 all-gather.6
  79.7 39.8 all-gather.8
  121.8 78.0 all-gather.10
  201.9 77.6 all-gather.12
  435.1 127.4 reduce-scatter.12
  566.0 69.5 reduce-scatter.6
  639.2 161.3 reduce-scatter.8
  804.1 161.1 reduce-scatter.10
  967.5 19.8 all-gather.14
  990.9 39.5 all-reduce.3
